TPU v7x, 32 devices: a whole 2x2x4 slice. The times are simulated.
32 devices in a mesh: parts: 2 (over y), lon: 4 (over z), lat: 2 (over core), chan: 2 (over x).
Axes of the slice: x: 2, y: 2, z: 4, core: 2. Of those that a mesh axis runs over, the one named last changes fastest.
Arguments:
- fine_act: bfloat16 [384, 896, 256], P(('parts', 'lat', 'chan'), 'lon'), parts along dimension 0, may hold values from -6 to 6
- coarse_grad: bfloat16 [192, 448, 128], P(('parts', 'lat'), 'lon', 'chan'), parts along dimension 0, may hold values from -6 to 6
- kernel: bfloat16 [3, 3, 256, 128], replicated, may hold values from -0.125 to 0.125
Outputs:
- input_grad: bfloat16 [384, 896, 256], P(('parts', 'lat', 'chan'), 'lon'), parts along dimension 0
- kernel_grad: float32 [6, 3, 256, 128], P('parts'), parts along dimension 0
There are 2 independent parts, one for each index of `parts`. A program takes and returns all parts, laid end to end along the dimension named above; an argument that names none is the same for every part. Nothing has to cross between parts.
All inputs are finite; a program needn't handle non-finite values.
Results may differ from a plain program's by a relative error of at most 0.001.
Values may be sent and summed in bfloat16 or wider, within the bound.
A program may use at most 64 MiB of HBM per device.

v0:
```python
import math

import jax
import jax.numpy as jnp
from jax import lax
from jax.sharding import PartitionSpec as P


def extended(shard, sides, width, wrap):
    for axis, dim in sides:
        peers, length = (lax.axis_size(axis), shard.shape[dim])
        up = [(i, (i + 1) % peers) for i in range(peers if wrap else peers - 1)]
        down = [(j, i) for i, j in up]
        last = lax.slice_in_dim(shard, length - width, length, axis=dim)
        leading = lax.slice_in_dim(shard, 0, width, axis=dim)
        before = lax.ppermute(last, axis, up)
        after = lax.ppermute(leading, axis, down)
        shard = jnp.concatenate([before, shard, after], axis=dim)
    return shard


def tap_slice(padded, tap_row, tap_col, first_row, row_count, col_count):
    return lax.dynamic_slice(
        padded, (first_row + 2 - tap_row, 2 - tap_col, 0), (row_count, col_count, padded.shape[2])
    )


def spread_zeros(even_grad):
    row_count, col_count, channels = even_grad.shape
    zero_rows = jnp.zeros_like(even_grad)
    doubled = jnp.stack([even_grad, zero_rows], axis=1).reshape(2 * row_count, col_count, channels)
    zero_cols = jnp.zeros_like(doubled)
    return jnp.stack([doubled, zero_cols], axis=2).reshape(2 * row_count, 2 * col_count, channels)


def on_device(fine_act, coarse_grad, kernel):
    even_act = fine_act[::2, ::2, :]
    half_rows, half_cols, in_width = even_act.shape
    out_width = kernel.shape[3]
    scale_factor = 1.0 / math.sqrt(
        half_rows * lax.axis_size(("lat", "chan")) * half_cols * lax.axis_size("lon")
    )
    even_flat = even_act.reshape(half_rows * half_cols, in_width)
    tiled = lax.all_to_all(coarse_grad, "chan", split_axis=0, concat_axis=2, tiled=True)
    widened = extended(tiled, (("lon", 1),), 1, True)
    padded = extended(widened, ((("lat", "chan"), 0),), 1, False)
    shifted_taps = [
        tap_slice(padded, tap_row, tap_col, 0, half_rows, half_cols).reshape(
            half_rows * half_cols, out_width
        )
        for tap_row in range(3)
        for tap_col in range(3)
    ]
    total = jnp.zeros((half_rows * half_cols, in_width), jnp.float32)
    for tap_index in range(9):
        total = total + lax.dot_general(
            shifted_taps[tap_index],
            kernel[tap_index // 3, tap_index % 3],
            (((1,), (1,)), ((), ())),
            preferred_element_type=jnp.float32,
        )
    input_grad = spread_zeros(total.astype(jnp.bfloat16).reshape(half_rows, half_cols, in_width))
    terms = [
        lax.dot_general(
            even_flat, shifted, (((0,), (0,)), ((), ())), preferred_element_type=jnp.float32
        )
        for shifted in shifted_taps
    ]
    stacked = jnp.stack(terms).reshape(3, 3, in_width, out_width)
    summed = lax.psum(stacked, ("lon", "lat", "chan"))
    kernel_grad = summed * scale_factor
    return (input_grad, kernel_grad)


def solution(mesh):
    placed = (P(("parts", "lat", "chan"), "lon", None), P(("parts", "lat"), "lon", "chan"), P())
    return jax.shard_map(
        on_device,
        mesh=mesh,
        in_specs=placed,
        out_specs=(P(("parts", "lat", "chan"), "lon", None), P("parts", None, None, None)),
        check_vma=False,
    )
```

profile of v0, /device:TPU:0, one launch (start us, length us, event | category | flops | bytes accessed | tf_op | source)
XLA Modules:
  0.0 158.4 jit_solution(2495849806670586597)
XLA Ops:
  7.2 4.2 %all-to-all-start = ((bf16[48,112,64]{1,2,0:T(8,128)(2,1)}), bf16[48,112,64]{1,2,0:T(8,128)(2,1)S(1)}, u32[]{:S(2)}, u32[]{:S(2)}) async-start(bf16[48,112,64]{1,2,0:T(8,128)(2,1)} %param.4), calls=%async_computation | async-start | bytes 1572864 | tf_op jit(solution)/shard_map/all_to_all | solution.py:44
  11.4 12.3 %slice.63 = bf16[24,112,256]{2,1,0:T(8,128)(2,1)S(1)} slice(bf16[48,224,256]{2,1,0:T(8,128)(2,1)} %param.3), slice={[0:48:2], [0:224:2], [0:256:1]} | slice | bytes 2752512 | tf_op jit(solution)/shard_map/slice | solution.py:37
  23.7 0.9 copy.19
  24.6 1.5 copy.20
  26.1 2.5 %collective-permute-start = (bf16[24,1,128]{2,1,0:T(2,128)(2,1)S(1)}, bf16[24,1,128]{2,1,0:T(2,128)(2,1)S(1)}, u32[]{:S(2)}, u32[]{:S(2)}) collective-permute-start(bf16[24,1,128]{2,1,0:T(2,128)(2,1)S(1)} %get-tuple-element.16), channel_id=1, source_target_pairs={{0,4},{4,8},{8,12},{12,0},{1,5},{5,9},{9,13},{13,1},{2,6},{6,10},{... | collective-permute-start | bytes 18440 | tf_op jit(solution)/shard_map/ppermute | solution.py:16
  28.6 2.1 %collective-permute-start.1 = (bf16[24,1,128]{2,1,0:T(2,128)(2,1)S(1)}, bf16[24,1,128]{2,1,0:T(2,128)(2,1)S(1)}, u32[]{:S(2)}, u32[]{:S(2)}) collective-permute-start(bf16[24,1,128]{2,1,0:T(2,128)(2,1)S(1)} %get-tuple-element.17), channel_id=1, source_target_pairs={{4,0},{8,4},{12,8},{0,12},{5,1},{9,5},{13,9},{1,13},{6,2},{10,6},{... | collective-permute-start | bytes 18440 | tf_op jit(solution)/shard_map/ppermute | solution.py:17
  30.7 1.4 copy.34
  32.1 1.8 %reshape.45 = bf16[2688,128]{0,1:T(8,128)(2,1)S(1)} reshape(bf16[24,112,2,64]{1,0,3,2:T(8,128)(2,1)} %bitcast.150) | data formatting | bytes 1376256 | tf_op jit(solution)/shard_map/reshape | solution.py:48
  33.9 2.9 %fusion.17 = f32[2688,256]{1,0:T(8,128)} fusion(bf16[2688,128]{0,1:T(8,128)(2,1)S(1)} %reshape.45, bf16[3,3,256,128]{3,2,1,0:T(8,128)(2,1)} %param.5), kind=kOutput, calls=%fused_computation.38 | convolution fusion | flops 176160768 | bytes 3506176 | tf_op jit(solution)/shard_map/dot_general | solution.py:56
  36.9 1.3 collective-permute-start.2
  38.2 4.7 %collective-permute-start.3 = (bf16[1,114,128]{2,1,0:T(8,128)(2,1)S(1)}, bf16[1,114,128]{2,1,0:T(8,128)(2,1)S(1)}, u32[]{:S(2)}, u32[]{:S(2)}) collective-permute-start(bf16[1,114,128]{2,1,0:T(8,128)(2,1)S(1)} %get-tuple-element.13), channel_id=1, source_target_pairs={{0,1},{1,2},{2,3},{4,5},{5,6},{6,7},{8,9},{9,10},{10,11},{12,13},{... | collective-permute-start | bytes 87560 | tf_op jit(solution)/shard_map/ppermute | solution.py:16
  43.0 1.1 pad_maximum_fusion.1
  44.1 0.2 collective-permute-done.3
  44.3 0.4 pad_maximum_fusion
  44.7 0.4 fusion.11
  45.1 0.4 fusion.10
  45.6 0.4 fusion.9
  46.0 2.4 %fusion.39 = (bf16[24,112,128]{2,1,0:T(8,128)(2,1)S(1)}, bf16[24,112,128]{2,1,0:T(8,128)(2,1)}, bf16[24,112,128]{2,1,0:T(8,128)(2,1)}, bf16[24,112,128]{2,1,0:T(...) fusion(bf16[25,114,128]{2,1,0:T(8,128)(2,1)S(1)} %get-tuple-element.11, ...), kind=kLoop, calls=%fused_computation.63 | loop fusion | bytes 8257536 | tf_op jit(solution)/shard_map/dynamic_slice | solution.py:23
  48.3 0.4 fusion.8
  48.8 0.4 fusion.3
  49.1 0.4 fusion.7
  49.5 0.4 fusion.6
  49.9 0.4 fusion.5
  50.3 0.4 fusion.4
  50.8 0.0 copy-start.8
  50.8 1.0 copy-done.8
  51.8 2.8 %copy.28 = f32[3,3,256,128]{3,2,1,0:T(8,128)} copy(f32[3,3,256,128]{2,3,1,0:T(8,128)} %bitcast.158) | data formatting | bytes 2359296 | tf_op jit(solution)/shard_map/reshape | solution.py:69
  54.5 0.0 all-reduce.4.cloned.1.call-update
  54.6 0.5 fusion.21
  55.1 0.6 copy-done.6
  55.7 0.5 fusion.14
  56.2 0.6 copy-done.5
  56.8 0.5 convolution_add_fusion.5
  57.3 0.6 copy-done.4
  57.9 0.5 convolution_add_fusion.4
  58.4 1.2 copy-done
  59.7 0.1 copy-done.2
  59.8 0.5 fusion
  60.3 0.5 fusion.1
  60.9 0.6 copy-done.3
  61.4 0.5 convolution_add_fusion.1
  62.0 0.5 fusion.2
  62.5 0.3 stack.36
  62.8 0.9 copy.32
  63.8 0.7 stack.37.clone
  64.5 4.6 %copy.29 = bf16[48,224,256]{2,1,0:T(8,128)(2,1)} copy(bf16[48,224,256]{2,0,1:T(8,128)(2,1)S(1)} %bitcast.143) | data formatting | bytes 11010048
  69.0 80.1 %all-reduce.4.cloned.1.call-done = f32[3,3,256,128]{3,2,1,0:T(8,128)} async-done(((f32[3,3,256,128]{3,2,1,0:T(8,128)}), f32[3,3,256,128]{3,2,1,0:T(8,128)}) %all-reduce.4.cloned.1.call-update) | async-done | bytes 1179664 | tf_op jit(solution)/shard_map/psum | solution.py:70
  149.2 2.4 %broadcast_multiply_fusion = f32[3,3,256,128]{3,2,1,0:T(8,128)} fusion(f32[3,3,256,128]{3,2,1,0:T(8,128)} %all-reduce.4.cloned.1.call-done), kind=kLoop, calls=%fused_computation.32 | loop fusion | flops 294912 | bytes 2359296 | tf_op jit(solution)/shard_map/mul | solution.py:71
  (23 shorter events, 0.1 us)
Async XLA Ops:
  7.2 16.5 %all-to-all-start = ((bf16[48,112,64]{1,2,0:T(8,128)(2,1)}), bf16[48,112,64]{1,2,0:T(8,128)(2,1)S(1)}, u32[]{:S(2)}, u32[]{:S(2)}) async-start(bf16[48,112,64]{1,2,0:T(8,128)(2,1)} %param.4), calls=%async_computation | async-start | bytes 1572864 | tf_op jit(solution)/shard_map/all_to_all | solution.py:44
  11.4 137.8 %all-reduce.4.cloned.1.call-start = ((), (), s32[]{:S(2)}) async-start(), calls=%async_computation.1 | async-start | bytes 2359296 | tf_op jit(solution)/shard_map/psum | solution.py:70
  26.1 10.7 %collective-permute-start = (bf16[24,1,128]{2,1,0:T(2,128)(2,1)S(1)}, bf16[24,1,128]{2,1,0:T(2,128)(2,1)S(1)}, u32[]{:S(2)}, u32[]{:S(2)}) collective-permute-start(bf16[24,1,128]{2,1,0:T(2,128)(2,1)S(1)} %get-tuple-element.16), channel_id=1, source_target_pairs={{0,4},{4,8},{8,12},{12,0},{1,5},{5,9},{9,13},{13,1},{2,6},{6,10},{... | collective-permute-start | bytes 18440 | tf_op jit(solution)/shard_map/ppermute | solution.py:16
  28.6 8.3 %collective-permute-start.1 = (bf16[24,1,128]{2,1,0:T(2,128)(2,1)S(1)}, bf16[24,1,128]{2,1,0:T(2,128)(2,1)S(1)}, u32[]{:S(2)}, u32[]{:S(2)}) collective-permute-start(bf16[24,1,128]{2,1,0:T(2,128)(2,1)S(1)} %get-tuple-element.17), channel_id=1, source_target_pairs={{4,0},{8,4},{12,8},{0,12},{5,1},{9,5},{13,9},{1,13},{6,2},{10,6},{... | collective-permute-start | bytes 18440 | tf_op jit(solution)/shard_map/ppermute | solution.py:17
  36.9 1.3 copy-start.10
  36.9 7.2 %collective-permute-start.2 = (bf16[1,114,128]{2,1,0:T(8,128)(2,1)S(1)}, bf16[1,114,128]{2,1,0:T(8,128)(2,1)S(1)}, u32[]{:S(2)}, u32[]{:S(2)}) collective-permute-start(bf16[1,114,128]{2,1,0:T(8,128)(2,1)S(1)} %get-tuple-element.12), channel_id=1, source_target_pairs={{1,0},{2,1},{3,2},{5,4},{6,5},{7,6},{9,8},{10,9},{11,10},{13,12},{... | collective-permute-start | bytes 87560 | tf_op jit(solution)/shard_map/ppermute | solution.py:17
  38.2 6.1 %collective-permute-start.3 = (bf16[1,114,128]{2,1,0:T(8,128)(2,1)S(1)}, bf16[1,114,128]{2,1,0:T(8,128)(2,1)S(1)}, u32[]{:S(2)}, u32[]{:S(2)}) collective-permute-start(bf16[1,114,128]{2,1,0:T(8,128)(2,1)S(1)} %get-tuple-element.13), channel_id=1, source_target_pairs={{0,1},{1,2},{2,3},{4,5},{5,6},{6,7},{8,9},{9,10},{10,11},{12,13},{... | collective-permute-start | bytes 87560 | tf_op jit(solution)/shard_map/ppermute | solution.py:16
  43.0 1.4 copy-start.11
  44.1 4.2 %copy-start.1 = (bf16[24,112,128]{2,1,0:T(8,128)(2,1)}, bf16[24,112,128]{2,1,0:T(8,128)(2,1)S(1)}, u32[]{:S(2)}) copy-start(bf16[24,112,128]{2,1,0:T(8,128)(2,1)S(1)} %get-tuple-element.15) | copy-start | bytes 2064388
  50.8 1.0 copy-start.8
  51.8 2.8 %copy-start.7 = (bf16[24,112,128]{2,1,0:T(8,128)(2,1)S(1)}, bf16[24,112,128]{2,1,0:T(8,128)(2,1)}, u32[]{:S(2)}) copy-start(bf16[24,112,128]{2,1,0:T(8,128)(2,1)} %get-tuple-element.19) | copy-start | bytes 2064388
  51.8 2.8 %copy-start.9 = (bf16[3,3,256,128]{3,2,1,0:T(8,128)(2,1)S(1)}, bf16[3,3,256,128]{3,2,1,0:T(8,128)(2,1)}, u32[]{:S(2)}) copy-start(bf16[3,3,256,128]{3,2,1,0:T(8,128)(2,1)} %param.5) | copy-start | bytes 1769476
  54.6 1.1 copy-start.6
  55.7 1.1 copy-start.5
  56.8 1.1 copy-start.4
  57.9 1.8 %copy-start = (f32[2688,256]{1,0:T(8,128)S(1)}, f32[2688,256]{1,0:T(8,128)}, u32[]{:S(2)}) copy-start(f32[2688,256]{1,0:T(8,128)} %fusion.17) | copy-start | bytes 8257540
  57.9 1.9 %copy-start.2 = (bf16[24,112,128]{2,1,0:T(8,128)(2,1)S(1)}, bf16[24,112,128]{2,1,0:T(8,128)(2,1)}, u32[]{:S(2)}) copy-start(bf16[24,112,128]{2,1,0:T(8,128)(2,1)} %copy-done.1) | copy-start | bytes 2064388
  60.3 1.1 copy-start.3
Sparse Core Ops, SparseCore 0:
  54.7 94.4 all-reduce.3
where the time goes:
time: 159 us; the launch traced here: 158 us
  waiting for transfers between devices  80.4 us (51%)
  local copies, waits for them, and re-layouts  34.3 us (22%)
  starting transfers between devices  14.8 us (9%)
  between operations  14.3 us (9%)
  matrix products  10.7 us (7%)
  other arithmetic  3.95 us (2%)
    psum x1, waiting for transfers between devices, on_device(): summed = lax.psum(stacked, ('lon', 'lat', 'chan'))  80.1 us
    slice x1, local copies, waits for them, and re-layouts, on_device(): even_act = fine_act[::2, ::2, :]  12.3 us
    unnamed x26, local copies, waits for them, and re-layouts  10.2 us
    ppermute x2, starting transfers between devices, extended(): before = lax.ppermute(last, axis, up)  7.2 us
    dot_general x9, matrix products, on_device(): lax.dot_general(shifted_taps[tap_index], kernel[tap_index // 3, tap_index...  7.09 us
    all_to_all x1, starting transfers between devices, on_device(): lax.all_to_all(coarse_grad, 'chan', split_axis=0, concat_axis=2, tiled=True)  4.25 us
    all_to_all x3, local copies, waits for them, and re-layouts, on_device(): lax.all_to_all(coarse_grad, 'chan', split_axis=0, concat_axis=2, tiled=True)  3.8 us
    dot_general x9, matrix products, on_device(): lax.dot_general(even_flat, shifted, (((0,), (0,)), ((), ())), preferred_e...  3.58 us
  transfers between devices with their start and end apart: 6, of which 2 were waited for; matrix products, arithmetic and copies ran while one was open for 19% of the time, Pallas kernels for 0%

commit v1 on v0

v1 whole, which is shorter than its diff:
```python
import functools
import math

import jax
import jax.numpy as jnp
from jax import lax
from jax.experimental import pallas as pl
from jax.experimental.pallas import tpu as pltpu
from jax.sharding import PartitionSpec as P

MESH = pl.DeviceIdType.MESH
LANES = 128
F32 = jnp.float32
BF16 = jnp.bfloat16
AXES = ("lon", "lat", "chan")


def one_hot(shape, test):
    rows = lax.broadcasted_iota(jnp.int32, shape, 0)
    cols = lax.broadcasted_iota(jnp.int32, shape, 1)
    return jnp.where(test(rows, cols), 1.0, 0.0).astype(BF16)


def share(rows, peers, unit):
    for size in range(unit, rows + 1, unit):
        if rows % size == 0 and rows // size <= peers:
            return size
    raise ValueError("no share")


def stage_plan(rows, order, sizes):
    plan = []
    for position, axis in enumerate(order):
        unit = 8
        for later in order[position + 1:]:
            unit *= sizes[later] if later != "lon" else 1
        part = share(rows, sizes[axis], unit)
        plan.append((axis, part, rows // part))
        rows = part
    return plan


def grads_kernel(
    sizes, half_rows, half_cols, out_ch, scale,
    fine, cg, kernel, eg_out, kg_out,
    fbuf, kcat, tiles, taps, even_t, edge_out, edge_in, acc, *rest,
):
    landing, (local_sem, tile_recv, tile_send, edge_send, edge_recv, red_send, red_recv, gat_send, gat_recv) = rest[:-9], rest[-9:]
    lon_n, lat_n, chan_n = (sizes[a] for a in AXES)
    me = {a: lax.axis_index(a) for a in AXES}
    lat, chan = me["lat"], me["chan"]
    h = half_rows
    width = cg.shape[1]
    in_ch = fbuf.shape[2]
    mine = pl.ds(pl.multiple_of(chan * width, width), width)

    def other(axis, step):
        return lax.rem(me[axis] + step, sizes[axis])

    local = [pltpu.make_async_copy(fine.at[:, 0], fbuf, local_sem.at[0])]
    for r in range(3):
        for s in range(3):
            local.append(
                pltpu.make_async_copy(
                    kernel.at[r, s], kcat.at[r, :, pl.ds(s * out_ch, out_ch)], local_sem.at[1 + 3 * r + s]
                )
            )
    for copy in local:
        copy.start()

    is_top = jnp.logical_and(lat == 0, chan == 0)
    is_bottom = jnp.logical_and(lat == lat_n - 1, chan == chan_n - 1)
    pltpu.make_async_copy(cg.at[pl.ds(chan * h, h)], tiles.at[pl.ds(1, h), mine], tile_recv.at[2]).start()

    @pl.when(chan > 0)
    def _():
        pltpu.make_async_copy(cg.at[chan * h - 1], tiles.at[0, mine], tile_recv.at[0]).start()

    @pl.when(chan < chan_n - 1)
    def _():
        pltpu.make_async_copy(cg.at[(chan + 1) * h], tiles.at[h + 1, mine], tile_recv.at[1]).start()

    barrier = pltpu.get_barrier_semaphore()
    greeted = 0
    for dl in range(lat_n):
        for dc in range(chan_n):
            if dl or dc:
                pl.semaphore_signal(
                    barrier, inc=1, device_id={"lat": other("lat", dl), "chan": other("chan", dc)}, device_id_type=MESH
                )
                greeted += 1
    for d in range(1, lon_n):
        pl.semaphore_signal(barrier, inc=1, device_id={"lon": other("lon", d)}, device_id_type=MESH)
        greeted += 1
    pl.semaphore_wait(barrier, greeted)

    sends = []

    def send(condition, src, dst, send_sem, recv_sem, where):
        copy = pltpu.make_async_remote_copy(
            src_ref=src, dst_ref=dst, send_sem=send_sem, recv_sem=recv_sem, device_id=where, device_id_type=MESH
        )
        if condition is None:
            copy.start()
        else:
            pl.when(condition)(lambda: copy.start())
        sends.append((condition, copy))

    slot = 0
    for d in range(1, chan_n):
        p = other("chan", d)
        send(p > 0, cg.at[jnp.maximum(p * h - 1, 0)], tiles.at[0, mine], tile_send.at[slot], tile_recv.at[0], {"chan": p})
        send(None, cg.at[pl.ds(p * h, h)], tiles.at[pl.ds(1, h), mine], tile_send.at[slot + 1], tile_recv.at[2], {"chan": p})
        send(
            p < chan_n - 1, cg.at[jnp.minimum((p + 1) * h, chan_n * h - 1)], tiles.at[h + 1, mine],
            tile_send.at[slot + 2], tile_recv.at[1], {"chan": p},
        )
        slot += 3
    send(
        lat < lat_n - 1, cg.at[chan_n * h - 1], tiles.at[0, mine], tile_send.at[slot], tile_recv.at[0],
        {"lat": jnp.minimum(lat + 1, lat_n - 1), "chan": 0},
    )
    send(
        lat > 0, cg.at[0], tiles.at[h + 1, mine], tile_send.at[slot + 1], tile_recv.at[1],
        {"lat": jnp.maximum(lat - 1, 0), "chan": chan_n - 1},
    )

    local[0].wait()
    pick = one_hot((2 * half_cols, LANES), lambda row, col: row == 2 * col)

    def take_even(i, _):
        picked = lax.dot_general(fbuf[i], pick, (((0,), (0,)), ((), ())), preferred_element_type=F32)
        even_t[:, pl.ds(pl.multiple_of(i * LANES, LANES), LANES)] = picked.astype(BF16)
        return 0

    lax.fori_loop(0, h, take_even, 0)

    @pl.when(is_top)
    def _():
        tiles[0] = jnp.zeros(tiles.shape[1:], BF16)

    @pl.when(is_bottom)
    def _():
        tiles[h + 1] = jnp.zeros(tiles.shape[1:], BF16)

    @pl.when(jnp.logical_not(is_top))
    def _():
        pltpu.make_async_copy(tiles.at[0], tiles.at[0], tile_recv.at[0]).wait()

    @pl.when(jnp.logical_not(is_bottom))
    def _():
        pltpu.make_async_copy(tiles.at[h + 1], tiles.at[h + 1], tile_recv.at[1]).wait()

    pltpu.make_async_copy(tiles.at[pl.ds(1, h)], tiles.at[pl.ds(1, h)], tile_recv.at[2]).wait()

    def shifted_source(row, col):
        s, j = col // LANES, col % LANES
        return jnp.logical_and(row == j + 1 - s, j < half_cols)

    shift = one_hot((half_cols, 3 * LANES), shifted_source)

    def build(k, edges):
        tile = tiles[k]
        moved = jnp.dot(tile, shift, preferred_element_type=F32).astype(BF16)
        at = pl.ds(pl.multiple_of(k * LANES, LANES), LANES)
        for s in range(3):
            taps[pl.ds(s * out_ch, out_ch), at] = moved[:, s * LANES:(s + 1) * LANES]
        last = one_hot(
            (half_cols, 2 * LANES),
            lambda row, col: jnp.logical_or(
                jnp.logical_and(row == half_cols - 1, col == k), jnp.logical_and(row == 0, col == k + LANES)
            ),
        )
        return edges + jnp.dot(tile, last, preferred_element_type=F32)

    edges = lax.fori_loop(0, h + 2, build, jnp.zeros((out_ch, 2 * LANES), F32)).astype(BF16)
    edge_out[0] = edges[:, :LANES]
    edge_out[1] = edges[:, LANES:]
    send(None, edge_out.at[0], edge_in.at[0], edge_send.at[0], edge_recv.at[0], {"lon": other("lon", 1)})
    send(None, edge_out.at[1], edge_in.at[1], edge_send.at[1], edge_recv.at[1], {"lon": other("lon", lon_n - 1)})
    for side in range(2):
        pltpu.make_async_copy(edge_in.at[side], edge_in.at[side], edge_recv.at[side]).wait()

    def inject(k, _):
        at = pl.ds(pl.multiple_of(k * LANES, LANES), LANES)
        for side, s, lane in ((1, 0, half_cols - 1), (0, 2, 0)):
            spot = one_hot((LANES, LANES), lambda row, col: jnp.logical_and(row == k, col == lane))
            block = taps[pl.ds(s * out_ch, out_ch), at].astype(F32)
            block = block + jnp.dot(edge_in[side], spot, preferred_element_type=F32)
            taps[pl.ds(s * out_ch, out_ch), at] = block.astype(BF16)
        return 0

    lax.fori_loop(0, h + 2, inject, 0)

    for r in range(3):
        part = lax.dot_general(
            even_t[...], taps[:, (2 - r) * LANES:(2 - r + h) * LANES], (((1,), (1,)), ((), ())), preferred_element_type=F32
        )
        for s in range(3):
            acc[pl.ds((3 * r + s) * in_ch, in_ch), :] = part[:, s * out_ch:(s + 1) * out_ch]

    streams = reduce_streams(acc.shape[0], sizes)
    bases = [base for base, _ in streams]
    stacks = [[] for _ in streams]
    counter = {"red": 0, "gat": 0, "land": 0}

    def started(stage):
        begun = []
        for index, (_, plan) in enumerate(streams):
            axis, part, owners = plan[stage]
            base = bases[index]
            land = landing[counter["land"]]
            counter["land"] += 1
            amowner = me[axis] < owners if owners < sizes[axis] else None
            arrivals = []
            for d in range(1, sizes[axis]):
                p = other(axis, d)
                n = counter["red"]
                counter["red"] += 1
                toowner = p < owners if owners < sizes[axis] else None
                target = p if toowner is None else jnp.minimum(p, owners - 1)
                send(
                    toowner, acc.at[pl.ds(pl.multiple_of(base + target * part, 8), part)], land.at[d - 1],
                    red_send.at[n], red_recv.at[n], {axis: p},
                )
                arrivals.append(n)
            own = me[axis] if amowner is None else jnp.minimum(me[axis], owners - 1)
            bases[index] = base + own * part
            stacks[index].append((axis, part, owners, base, amowner))
            begun.append((index, land, arrivals, amowner, part))
        return begun

    def finished(begun, final):
        for index, land, arrivals, amowner, part in begun:
            at = pl.ds(pl.multiple_of(bases[index], 8), part)

            def absorb():
                for position, n in enumerate(arrivals):
                    pltpu.make_async_copy(land.at[position], land.at[position], red_recv.at[n]).wait()
                total = acc[at, :]
                for position in range(len(arrivals)):
                    total = total + land[position]
                if final:
                    kg_out[at, :] = total * scale
                else:
                    acc[at, :] = total

            if amowner is None:
                absorb()
            else:
                pl.when(amowner)(absorb)

    begun = started(0)
    finished(begun, False)
    begun = started(1)

    for copy in local[1:]:
        copy.wait()

    def make_even_grad(i, _):
        total = jnp.zeros((in_ch, 2 * LANES), F32)
        for r in range(3):
            at = pl.ds(pl.multiple_of(i * 2 * LANES + (2 - r) * LANES, LANES), 2 * LANES)
            total = total + jnp.dot(kcat[r], taps[:, at], preferred_element_type=F32)
        eg_out[:, pl.ds(pl.multiple_of(i * 2 * LANES, LANES), 2 * LANES)] = total.astype(BF16)
        return 0

    lax.fori_loop(0, h // 2, make_even_grad, 0)

    finished(begun, False)
    begun = started(2)
    finished(begun, True)

    for stage in (2, 1, 0):
        waits = []
        for index in range(len(streams)):
            axis, part, owners, base, amowner = stacks[index][stage]
            own = me[axis] if amowner is None else jnp.minimum(me[axis], owners - 1)
            at = pl.ds(pl.multiple_of(base + own * part, 8), part)
            for d in range(1, sizes[axis]):
                n = counter["gat"]
                counter["gat"] += 1
                send(amowner, kg_out.at[at], kg_out.at[at], gat_send.at[n], gat_recv.at[n], {axis: other(axis, d)})
                q = other(axis, sizes[axis] - d)
                fromowner = q < owners if owners < sizes[axis] else None
                source = q if fromowner is None else jnp.minimum(q, owners - 1)
                there = kg_out.at[pl.ds(pl.multiple_of(base + source * part, 8), part)]
                waits.append((fromowner, pltpu.make_async_copy(there, there, gat_recv.at[n])))
        for condition, copy in waits:
            if condition is None:
                copy.wait()
            else:
                pl.when(condition)(lambda copy=copy: copy.wait())

    for condition, copy in sends:
        if condition is None:
            copy.wait_send()
        else:
            pl.when(condition)(lambda copy=copy: copy.wait_send())


def reduce_streams(rows, sizes):
    half = rows // sizes["lat"] // 2
    streams = []
    for index, order in enumerate((("lon", "chan"), ("chan", "lon"))):
        plan = [("lat", half, sizes["lat"])] + stage_plan(half, order, sizes)
        streams.append((index * half * sizes["lat"], plan))
    return streams


def spread_kernel(half_cols, eg, out):
    spread = one_hot((2 * half_cols, LANES), lambda row, col: row == 2 * col)
    for k in range(out.shape[0] // 2):
        row = lax.dot_general(
            spread, eg[:, k * LANES:(k + 1) * LANES], (((1,), (1,)), ((), ())), preferred_element_type=F32
        )
        out[2 * k] = row.astype(BF16)
        out[2 * k + 1] = jnp.zeros(out.shape[1:], BF16)


def on_device(sizes, fine_act, coarse_grad, kernel):
    fine_rows, fine_cols, in_ch = fine_act.shape
    out_ch = kernel.shape[3]
    h, w = fine_rows // 2, fine_cols // 2
    lon_n, lat_n, chan_n = (sizes[a] for a in AXES)
    scale = 1.0 / math.sqrt(h * lat_n * chan_n * w * lon_n)
    cg = jnp.transpose(coarse_grad, (0, 2, 1))
    fine = fine_act.reshape(h, 2, fine_cols, in_ch)
    streams = reduce_streams(9 * in_ch, sizes)
    landing, count = [], 0
    for stage in range(3):
        for _, plan in streams:
            axis, part, _ = plan[stage]
            landing.append(pltpu.VMEM((sizes[axis] - 1, part, out_ch), F32))
            count += sizes[axis] - 1
    dma = pltpu.SemaphoreType.DMA
    vmem = pl.BlockSpec(memory_space=pltpu.VMEM)
    hbm = pl.BlockSpec(memory_space=pl.ANY)
    eg, kg = pl.pallas_call(
        functools.partial(grads_kernel, sizes, h, w, out_ch, scale),
        out_shape=(
            jax.ShapeDtypeStruct((in_ch, h * LANES), BF16),
            jax.ShapeDtypeStruct((9 * in_ch, out_ch), F32),
        ),
        in_specs=[hbm, hbm, hbm],
        out_specs=(vmem, vmem),
        scratch_shapes=[
            pltpu.VMEM((h, fine_cols, in_ch), BF16),
            pltpu.VMEM((3, in_ch, 3 * out_ch), BF16),
            pltpu.VMEM((h + 2, out_ch, w), BF16),
            pltpu.VMEM((3 * out_ch, (h + 2) * LANES), BF16),
            pltpu.VMEM((in_ch, h * LANES), BF16),
            pltpu.VMEM((2, out_ch, LANES), BF16),
            pltpu.VMEM((2, out_ch, LANES), BF16),
            pltpu.VMEM((9 * in_ch, out_ch), F32),
            *landing,
            dma((10,)),
            dma((3,)),
            dma((3 * (chan_n - 1) + 2,)),
            dma((2,)),
            dma((2,)),
            dma((count,)),
            dma((count,)),
            dma((count,)),
            dma((count,)),
        ],
        compiler_params=pltpu.CompilerParams(
            collective_id=0, has_side_effects=True, vmem_limit_bytes=40 * 1024 * 1024
        ),
        name="grads",
    )(fine, cg, kernel)
    step = 4 if h % 4 == 0 else 1
    input_grad = pl.pallas_call(
        functools.partial(spread_kernel, w),
        out_shape=jax.ShapeDtypeStruct(fine_act.shape, BF16),
        grid=(h // step,),
        in_specs=[pl.BlockSpec((in_ch, step * LANES), lambda i: (0, i))],
        out_specs=pl.BlockSpec((2 * step, fine_cols, in_ch), lambda i: (i, 0, 0)),
        name="spread",
    )(eg)
    return (input_grad, kg.reshape(3, 3, in_ch, out_ch))


def solution(mesh):
    placed = (P(("parts", "lat", "chan"), "lon", None), P(("parts", "lat"), "lon", "chan"), P())
    sizes = {axis: mesh.shape[axis] for axis in AXES}
    return jax.shard_map(
        functools.partial(on_device, sizes),
        mesh=mesh,
        in_specs=placed,
        out_specs=(P(("parts", "lat", "chan"), "lon", None), P("parts", None, None, None)),
        check_vma=False,
    )
```

time: 159 us -> 71.6 us (0.45)
  waiting for transfers between devices: 80.4 us -> 0 us
  Pallas kernels: 0 us -> 63.7 us
  local copies, waits for them, and re-layouts: 34.3 us -> 6.92 us
  starting transfers between devices: 14.8 us -> 0 us
  between operations: 14.3 us -> 0.66 us
  matrix products: 10.7 us -> 0 us
  other arithmetic: 3.95 us -> 0 us
    psum x1 -> x0, waiting for transfers between devices: 80.1 us -> none  [on_device(): summed = lax.psum(stacked, ('lon', 'lat', 'chan'))]
    pallas_call x0 -> x2, Pallas kernels: none -> 63.7 us  [the longest x1 57.8 us: on_device(): pl.pallas_call(functools.partial(grads_kernel, sizes, h, w, out_ch, scale...]
    slice x2 -> x0, local copies, waits for them, and re-layouts: 12.3 us -> none  [the longest x1 12.3 us: on_device(): even_act = fine_act[::2, ::2, :]]
    dot_general x18 -> x0, matrix products: 10.7 us -> none  [the longest x9 7.09 us: on_device(): lax.dot_general(shifted_taps[tap_index], kernel[tap_index // 3, tap_index...]
    ppermute x4 -> x0, starting transfers between devices: 10.6 us -> none  [the longest x2 7.2 us: extended(): before = lax.ppermute(last, axis, up)]
    reshape x2 -> x0, local copies, waits for them, and re-layouts: 4.59 us -> none  [the longest x1 2.76 us: on_device(): stacked = jnp.stack(terms).reshape(3, 3, in_width, out_width)]
    all_to_all x1 -> x0, starting transfers between devices: 4.25 us -> none  [on_device(): lax.all_to_all(coarse_grad, 'chan', split_axis=0, concat_axis=2, tiled=True)]
    all_to_all x3 -> x0, local copies, waits for them, and re-layouts: 3.8 us -> none  [on_device(): lax.all_to_all(coarse_grad, 'chan', split_axis=0, concat_axis=2, tiled=True)]
  transfers between devices with their start and end apart: 6 -> 0, of which waited for: 2 -> 0; matrix products, arithmetic and copies ran while one was open for 19% -> 0% of each run, Pallas kernels for 0% -> 0%
where the time goes in v1:
time: 71.6 us; the launch traced here: 71.3 us
  Pallas kernels  63.7 us (89%)
  local copies, waits for them, and re-layouts  6.92 us (10%)
    pallas_call x1, Pallas kernels, on_device(): pl.pallas_call(functools.partial(grads_kernel, sizes, h, w, out_ch, scale...  57.8 us
    unnamed x9, local copies, waits for them, and re-layouts  6.92 us
    pallas_call x1, Pallas kernels, on_device(): pl.pallas_call(functools.partial(spread_kernel, w), out_shape=jax.ShapeDt...  5.91 us

profile of v1, /device:TPU:0, one launch (start us, length us, event | category | flops | bytes accessed | tf_op | source)
XLA Modules:
  0.0 71.3 jit_solution(3975460231153973070)
XLA Ops:
  0.6 0.0 copy-start
  0.6 2.6 %copy-done = bf16[48,224,256]{2,1,0:T(8,128)(2,1)S(1)} copy-done((bf16[48,224,256]{2,1,0:T(8,128)(2,1)S(1)}, bf16[48,224,256]{2,1,0:T(8,128)(2,1)}, u32[]{:S(2)}) %copy-start) | copy-done | bytes 5505048
  3.2 0.0 copy-start.2
  3.2 1.1 %copy-done.2 = bf16[48,112,64]{1,2,0:T(8,128)(2,1)S(1)} copy-done((bf16[48,112,64]{1,2,0:T(8,128)(2,1)S(1)}, bf16[48,112,64]{1,2,0:T(8,128)(2,1)}, u32[]{:S(2)}) %copy-start.2) | copy-done | bytes 688152
  4.3 0.0 copy-start.3
  4.3 1.1 %copy-done.3 = bf16[3,3,256,128]{3,2,1,0:T(8,128)(2,1)S(1)} copy-done((bf16[3,3,256,128]{3,2,1,0:T(8,128)(2,1)S(1)}, bf16[3,3,256,128]{3,2,1,0:T(8,128)(2,1)}, u32[]{:S(2)}) %copy-start.3) | copy-done | bytes 589848
  5.4 57.8 %grads.1 = (bf16[256,3072]{1,0:T(8,128)(2,1)S(1)}, f32[2304,128]{1,0:T(8,128)S(1)}) custom-call(bf16[24,2,224,256]{3,2,1,0:T(8,128)(2,1)S(1)} %bitcast.3, bf16[48,64,112]{2,1,0:T(8,128)(2,1)S(1)} %bitcast.5, bf16[3,3,256,128]{3,2,1,0:T(8,128)(2,1)S(1)} %copy-done.3), custom_call_target="tpu_custom_call" | custom-call | tf_op jit(solution)/shard_map/grads/pallas_call | solution.py:339
  63.2 0.0 copy-start.1
  63.2 1.2 %copy-done.1 = bf16[256,3072]{1,0:T(8,128)(2,1)} copy-done((bf16[256,3072]{1,0:T(8,128)(2,1)}, bf16[256,3072]{1,0:T(8,128)(2,1)S(1)}, u32[]{:S(2)}) %copy-start.1) | copy-done | bytes 1572888
  64.4 5.9 %spread.1 = bf16[48,224,256]{2,1,0:T(8,128)(2,1)} custom-call(bf16[256,3072]{1,0:T(8,128)(2,1)} %copy-done.1), custom_call_target="tpu_custom_call" | custom-call | tf_op jit(solution)/shard_map/spread/pallas_call | solution.py:373
  70.3 1.0 %copy.6 = f32[3,3,256,128]{3,2,1,0:T(8,128)} copy(f32[3,3,256,128]{3,2,1,0:T(8,128)S(1)} %bitcast.4) | data formatting | bytes 2359296
Async XLA Ops:
  0.6 2.6 %copy-start = (bf16[48,224,256]{2,1,0:T(8,128)(2,1)S(1)}, bf16[48,224,256]{2,1,0:T(8,128)(2,1)}, u32[]{:S(2)}) copy-start(bf16[48,224,256]{2,1,0:T(8,128)(2,1)} %param.3) | copy-start | bytes 16515076
  3.2 1.1 %copy-start.2 = (bf16[48,112,64]{1,2,0:T(8,128)(2,1)S(1)}, bf16[48,112,64]{1,2,0:T(8,128)(2,1)}, u32[]{:S(2)}) copy-start(bf16[48,112,64]{1,2,0:T(8,128)(2,1)} %param.4) | copy-start | bytes 2064388
  4.3 1.1 %copy-start.3 = (bf16[3,3,256,128]{3,2,1,0:T(8,128)(2,1)S(1)}, bf16[3,3,256,128]{3,2,1,0:T(8,128)(2,1)}, u32[]{:S(2)}) copy-start(bf16[3,3,256,128]{3,2,1,0:T(8,128)(2,1)} %kernel.1) | copy-start | bytes 1769476
  63.2 1.2 %copy-start.1 = (bf16[256,3072]{1,0:T(8,128)(2,1)}, bf16[256,3072]{1,0:T(8,128)(2,1)S(1)}, u32[]{:S(2)}) copy-start(bf16[256,3072]{1,0:T(8,128)(2,1)S(1)} %get-tuple-element.4.eg) | copy-start | bytes 4718596

commit v2 on v1

--- a/solution.py
+++ b/solution.py
@@ -42,8 +42,8 @@
 
 def grads_kernel(
     sizes, half_rows, half_cols, out_ch, scale,
-    fine, cg, kernel, eg_out, kg_out,
-    fbuf, kcat, tiles, taps, even_t, edge_out, edge_in, acc, *rest,
+    fine, cg, kernel, rows_out, kg_out,
+    fbuf, kcat, tiles, taps, even_t, edge_out, edge_in, acc, rows_buf, row_sem, *rest,
 ):
     landing, (local_sem, tile_recv, tile_send, edge_send, edge_recv, red_send, red_recv, gat_send, gat_recv) = rest[:-9], rest[-9:]
     lon_n, lat_n, chan_n = (sizes[a] for a in AXES)
@@ -192,106 +192,143 @@
 
     lax.fori_loop(0, h + 2, inject, 0)
 
-    for r in range(3):
+    counter = {"red": 0, "gat": 0, "land": 0}
+    blocks = reduce_blocks(acc.shape[0], sizes)
+    state = []
+
+    def weight_terms(r):
         part = lax.dot_general(
             even_t[...], taps[:, (2 - r) * LANES:(2 - r + h) * LANES], (((1,), (1,)), ((), ())), preferred_element_type=F32
         )
         for s in range(3):
             acc[pl.ds((3 * r + s) * in_ch, in_ch), :] = part[:, s * out_ch:(s + 1) * out_ch]
 
-    streams = reduce_streams(acc.shape[0], sizes)
-    bases = [base for base, _ in streams]
-    stacks = [[] for _ in streams]
-    counter = {"red": 0, "gat": 0, "land": 0}
-
-    def started(stage):
-        begun = []
-        for index, (_, plan) in enumerate(streams):
-            axis, part, owners = plan[stage]
-            base = bases[index]
-            land = landing[counter["land"]]
-            counter["land"] += 1
-            amowner = me[axis] < owners if owners < sizes[axis] else None
-            arrivals = []
-            for d in range(1, sizes[axis]):
-                p = other(axis, d)
-                n = counter["red"]
-                counter["red"] += 1
-                toowner = p < owners if owners < sizes[axis] else None
-                target = p if toowner is None else jnp.minimum(p, owners - 1)
-                send(
-                    toowner, acc.at[pl.ds(pl.multiple_of(base + target * part, 8), part)], land.at[d - 1],
-                    red_send.at[n], red_recv.at[n], {axis: p},
-                )
-                arrivals.append(n)
-            own = me[axis] if amowner is None else jnp.minimum(me[axis], owners - 1)
-            bases[index] = base + own * part
-            stacks[index].append((axis, part, owners, base, amowner))
-            begun.append((index, land, arrivals, amowner, part))
-        return begun
-
-    def finished(begun, final):
-        for index, land, arrivals, amowner, part in begun:
-            at = pl.ds(pl.multiple_of(bases[index], 8), part)
-
-            def absorb():
-                for position, n in enumerate(arrivals):
-                    pltpu.make_async_copy(land.at[position], land.at[position], red_recv.at[n]).wait()
-                total = acc[at, :]
-                for position in range(len(arrivals)):
-                    total = total + land[position]
-                if final:
-                    kg_out[at, :] = total * scale
-                else:
-                    acc[at, :] = total
-
-            if amowner is None:
-                absorb()
+    def owner_of(index, axis, owners):
+        if owners == sizes[axis]:
+            return None, index
+        return index < owners, jnp.minimum(index, owners - 1)
+
+    def scatter(block, stage):
+        start, plan = blocks[block]
+        axis, part, owners = plan[stage]
+        base = start if stage == 0 else state[block]["base"]
+        if stage == 0:
+            state.append({"stack": []})
+        land = landing[counter["land"]]
+        counter["land"] += 1
+        arrivals = []
+        for d in range(1, sizes[axis]):
+            p = other(axis, d)
+            n = counter["red"]
+            counter["red"] += 1
+            toowner, target = owner_of(p, axis, owners)
+            send(
+                toowner, acc.at[pl.ds(pl.multiple_of(base + target * part, 8), part)], land.at[d - 1],
+                red_send.at[n], red_recv.at[n], {axis: p},
+            )
+            arrivals.append(n)
+        amowner, own = owner_of(me[axis], axis, owners)
+        state[block]["base"] = base + own * part
+        state[block]["stack"].append((axis, part, owners, base, amowner, own))
+        state[block]["open"] = (land, arrivals, amowner, part)
+
+    def add_up(block, final=False):
+        land, arrivals, amowner, part = state[block]["open"]
+        at = pl.ds(pl.multiple_of(state[block]["base"], 8), part)
+
+        def absorb():
+            for position, n in enumerate(arrivals):
+                pltpu.make_async_copy(land.at[position], land.at[position], red_recv.at[n]).wait()
+            total = acc[at, :]
+            for position in range(len(arrivals)):
+                total = total + land[position]
+            if final:
+                kg_out[at, :] = total * scale
             else:
-                pl.when(amowner)(absorb)
-
-    begun = started(0)
-    finished(begun, False)
-    begun = started(1)
-
-    for copy in local[1:]:
-        copy.wait()
+                acc[at, :] = total
+
+        if amowner is None:
+            absorb()
+        else:
+            pl.when(amowner)(absorb)
+
+    def gather(block, stage):
+        axis, part, owners, base, amowner, own = state[block]["stack"][stage]
+        at = pl.ds(pl.multiple_of(base + own * part, 8), part)
+        waits = []
+        for d in range(1, sizes[axis]):
+            n = counter["gat"]
+            counter["gat"] += 1
+            send(amowner, kg_out.at[at], kg_out.at[at], gat_send.at[n], gat_recv.at[n], {axis: other(axis, d)})
+            fromowner, source = owner_of(other(axis, sizes[axis] - d), axis, owners)
+            there = kg_out.at[pl.ds(pl.multiple_of(base + source * part, 8), part)]
+            waits.append((fromowner, pltpu.make_async_copy(there, there, gat_recv.at[n])))
+        state[block]["waits"] = waits
+
+    def gathered(block):
+        for condition, copy in state[block]["waits"]:
+            if condition is None:
+                copy.wait()
+            else:
+                pl.when(condition)(lambda copy=copy: copy.wait())
+
+    spread = one_hot((2 * half_cols, LANES), lambda row, col: row == 2 * col)
 
     def make_even_grad(i, _):
         total = jnp.zeros((in_ch, 2 * LANES), F32)
         for r in range(3):
             at = pl.ds(pl.multiple_of(i * 2 * LANES + (2 - r) * LANES, LANES), 2 * LANES)
             total = total + jnp.dot(kcat[r], taps[:, at], preferred_element_type=F32)
-        eg_out[:, pl.ds(pl.multiple_of(i * 2 * LANES, LANES), 2 * LANES)] = total.astype(BF16)
+        total = total.astype(BF16)
+        for k in range(2):
+            row = lax.dot_general(
+                spread, total[:, k * LANES:(k + 1) * LANES], (((1,), (1,)), ((), ())), preferred_element_type=F32
+            )
+            rows_buf[2 * i + k] = row.astype(BF16)
         return 0
 
-    lax.fori_loop(0, h // 2, make_even_grad, 0)
-
-    finished(begun, False)
-    begun = started(2)
-    finished(begun, True)
-
-    for stage in (2, 1, 0):
-        waits = []
-        for index in range(len(streams)):
-            axis, part, owners, base, amowner = stacks[index][stage]
-            own = me[axis] if amowner is None else jnp.minimum(me[axis], owners - 1)
-            at = pl.ds(pl.multiple_of(base + own * part, 8), part)
-            for d in range(1, sizes[axis]):
-                n = counter["gat"]
-                counter["gat"] += 1
-                send(amowner, kg_out.at[at], kg_out.at[at], gat_send.at[n], gat_recv.at[n], {axis: other(axis, d)})
-                q = other(axis, sizes[axis] - d)
-                fromowner = q < owners if owners < sizes[axis] else None
-                source = q if fromowner is None else jnp.minimum(q, owners - 1)
-                there = kg_out.at[pl.ds(pl.multiple_of(base + source * part, 8), part)]
-                waits.append((fromowner, pltpu.make_async_copy(there, there, gat_recv.at[n])))
-        for condition, copy in waits:
-            if condition is None:
-                copy.wait()
-            else:
-                pl.when(condition)(lambda copy=copy: copy.wait())
-
+    pairs = h // 2
+    row_copies = []
+    cuts = [pairs * k // 4 for k in range(5)]
+
+    def even_grads(k):
+        lax.fori_loop(cuts[k], cuts[k + 1], make_even_grad, 0)
+        at = pl.ds(2 * cuts[k], 2 * (cuts[k + 1] - cuts[k]))
+        copy = pltpu.make_async_copy(rows_buf.at[at], rows_out.at[at], row_sem.at[k])
+        copy.start()
+        row_copies.append(copy)
+
+    weight_terms(0)
+    scatter(0, 0)
+    weight_terms(1)
+    add_up(0)
+    scatter(0, 1)
+    scatter(1, 0)
+    weight_terms(2)
+    add_up(1)
+    scatter(1, 1)
+    scatter(2, 0)
+    for copy in local[1:]:
+        copy.wait()
+    add_up(2)
+    scatter(2, 1)
+    even_grads(0)
+    for block in range(3):
+        add_up(block)
+        scatter(block, 2)
+        even_grads(block + 1)
+    for block in range(3):
+        add_up(block, True)
+        gather(block, 2)
+    for stage in (1, 0):
+        for block in range(3):
+            gathered(block)
+            gather(block, stage)
+    for block in range(3):
+        gathered(block)
+
+    for copy in row_copies:
+        copy.wait()
     for condition, copy in sends:
         if condition is None:
             copy.wait_send()
@@ -299,23 +336,36 @@
             pl.when(condition)(lambda copy=copy: copy.wait_send())
 
 
-def reduce_streams(rows, sizes):
-    half = rows // sizes["lat"] // 2
-    streams = []
-    for index, order in enumerate((("lon", "chan"), ("chan", "lon"))):
-        plan = [("lat", half, sizes["lat"])] + stage_plan(half, order, sizes)
-        streams.append((index * half * sizes["lat"], plan))
-    return streams
-
-
-def spread_kernel(half_cols, eg, out):
-    spread = one_hot((2 * half_cols, LANES), lambda row, col: row == 2 * col)
-    for k in range(out.shape[0] // 2):
-        row = lax.dot_general(
-            spread, eg[:, k * LANES:(k + 1) * LANES], (((1,), (1,)), ((), ())), preferred_element_type=F32
-        )
-        out[2 * k] = row.astype(BF16)
-        out[2 * k + 1] = jnp.zeros(out.shape[1:], BF16)
+def reduce_blocks(rows, sizes):
+    count = rows // 3
+    return [(block * count, stage_plan(count, ("lat", "chan", "lon"), sizes)) for block in range(3)]
+
+
+def finish_kernel(rows, kg_in, grad_out, kg_out, rows_buf, kg_buf, zeros, sems):
+    zero_rows = zeros.shape[0]
+    groups = rows.shape[0] // zero_rows
+    kg_read = pltpu.make_async_copy(kg_in, kg_buf, sems.at[0])
+    kg_write = pltpu.make_async_copy(kg_buf, kg_out, sems.at[1])
+    kg_read.start()
+    reads, writes = [], [kg_write]
+    for k in range(groups):
+        at = pl.ds(k * zero_rows, zero_rows)
+        reads.append(pltpu.make_async_copy(rows.at[at], rows_buf.at[at], sems.at[2 + 3 * k]))
+        reads[k].start()
+    zeros[...] = jnp.zeros(zeros.shape, BF16)
+    for k in range(groups):
+        at = pl.ds(k * zero_rows, zero_rows)
+        writes.append(pltpu.make_async_copy(zeros, grad_out.at[at, 1], sems.at[3 + 3 * k]))
+        writes[-1].start()
+    kg_read.wait()
+    kg_write.start()
+    for k in range(groups):
+        at = pl.ds(k * zero_rows, zero_rows)
+        reads[k].wait()
+        writes.append(pltpu.make_async_copy(rows_buf.at[at], grad_out.at[at, 0], sems.at[4 + 3 * k]))
+        writes[-1].start()
+    for copy in writes:
+        copy.wait()
 
 
 def on_device(sizes, fine_act, coarse_grad, kernel):
@@ -326,24 +376,23 @@
     scale = 1.0 / math.sqrt(h * lat_n * chan_n * w * lon_n)
     cg = jnp.transpose(coarse_grad, (0, 2, 1))
     fine = fine_act.reshape(h, 2, fine_cols, in_ch)
-    streams = reduce_streams(9 * in_ch, sizes)
+    blocks = reduce_blocks(9 * in_ch, sizes)
     landing, count = [], 0
-    for stage in range(3):
-        for _, plan in streams:
-            axis, part, _ = plan[stage]
-            landing.append(pltpu.VMEM((sizes[axis] - 1, part, out_ch), F32))
-            count += sizes[axis] - 1
+    for block, stage in ((0, 0), (0, 1), (1, 0), (1, 1), (2, 0), (2, 1), (0, 2), (1, 2), (2, 2)):
+        axis, part, _ = blocks[block][1][stage]
+        landing.append(pltpu.VMEM((sizes[axis] - 1, part, out_ch), F32))
+        count += sizes[axis] - 1
     dma = pltpu.SemaphoreType.DMA
     vmem = pl.BlockSpec(memory_space=pltpu.VMEM)
-    hbm = pl.BlockSpec(memory_space=pl.ANY)
-    eg, kg = pl.pallas_call(
+    hbm = pl.BlockSpec(memory_space=pltpu.HBM)
+    rows, kg = pl.pallas_call(
         functools.partial(grads_kernel, sizes, h, w, out_ch, scale),
         out_shape=(
-            jax.ShapeDtypeStruct((in_ch, h * LANES), BF16),
+            jax.ShapeDtypeStruct((h, fine_cols, in_ch), BF16),
             jax.ShapeDtypeStruct((9 * in_ch, out_ch), F32),
         ),
         in_specs=[hbm, hbm, hbm],
-        out_specs=(vmem, vmem),
+        out_specs=(hbm, vmem),
         scratch_shapes=[
             pltpu.VMEM((h, fine_cols, in_ch), BF16),
             pltpu.VMEM((3, in_ch, 3 * out_ch), BF16),
@@ -353,6 +402,8 @@
             pltpu.VMEM((2, out_ch, LANES), BF16),
             pltpu.VMEM((2, out_ch, LANES), BF16),
             pltpu.VMEM((9 * in_ch, out_ch), F32),
+            pltpu.VMEM((h, fine_cols, in_ch), BF16),
+            dma((4,)),
             *landing,
             dma((10,)),
             dma((3,)),
@@ -365,20 +416,29 @@
             dma((count,)),
         ],
         compiler_params=pltpu.CompilerParams(
-            collective_id=0, has_side_effects=True, vmem_limit_bytes=40 * 1024 * 1024
+            collective_id=0, has_side_effects=True, vmem_limit_bytes=60 * 1024 * 1024
         ),
         name="grads",
     )(fine, cg, kernel)
-    step = 4 if h % 4 == 0 else 1
-    input_grad = pl.pallas_call(
-        functools.partial(spread_kernel, w),
-        out_shape=jax.ShapeDtypeStruct(fine_act.shape, BF16),
-        grid=(h // step,),
-        in_specs=[pl.BlockSpec((in_ch, step * LANES), lambda i: (0, i))],
-        out_specs=pl.BlockSpec((2 * step, fine_cols, in_ch), lambda i: (i, 0, 0)),
-        name="spread",
-    )(eg)
-    return (input_grad, kg.reshape(3, 3, in_ch, out_ch))
+    zero_rows = math.gcd(h, 8)
+    input_grad, kernel_grad = pl.pallas_call(
+        finish_kernel,
+        out_shape=(
+            jax.ShapeDtypeStruct((h, 2, fine_cols, in_ch), BF16),
+            jax.ShapeDtypeStruct(kg.shape, F32),
+        ),
+        in_specs=[hbm, hbm],
+        out_specs=(hbm, hbm),
+        scratch_shapes=[
+            pltpu.VMEM((h, fine_cols, in_ch), BF16),
+            pltpu.VMEM(kg.shape, F32),
+            pltpu.VMEM((zero_rows, fine_cols, in_ch), BF16),
+            dma((2 + 3 * (h // zero_rows),)),
+        ],
+        compiler_params=pltpu.CompilerParams(vmem_limit_bytes=60 * 1024 * 1024),
+        name="finish",
+    )(rows, kg)
+    return (input_grad.reshape(fine_act.shape), kernel_grad.reshape(3, 3, in_ch, out_ch))
 
 
 def solution(mesh):

time: 71.6 us -> 62.3 us (0.87)
  local copies, waits for them, and re-layouts: 6.92 us -> 0 us
  Pallas kernels: 63.7 us -> 61.5 us
    unnamed x9 -> x0, local copies, waits for them, and re-layouts: 6.92 us -> none
    pallas_call x1, Pallas kernels: 5.91 us -> 4.6 us  [on_device(): pl.pallas_call(finish_kernel, out_shape=(jax.ShapeDtypeStruct((h, 2, fine...]
    pallas_call x1, Pallas kernels: 57.8 us -> 56.9 us  [on_device(): pl.pallas_call(functools.partial(grads_kernel, sizes, h, w, out_ch, scale...]
where the time goes in v2:
time: 62.3 us; the launch traced here: 62.2 us
  Pallas kernels  61.5 us (99%)
  between operations  0.64 us (1%)
    pallas_call x1, Pallas kernels, on_device(): pl.pallas_call(functools.partial(grads_kernel, sizes, h, w, out_ch, scale...  56.9 us
    pallas_call x1, Pallas kernels, on_device(): pl.pallas_call(finish_kernel, out_shape=(jax.ShapeDtypeStruct((h, 2, fine...  4.6 us

profile of v2, /device:TPU:0, one launch (start us, length us, event | category | flops | bytes accessed | tf_op | source)
XLA Modules:
  0.0 62.2 jit_solution(429622020933978109)
XLA Ops:
  0.6 56.9 %grads.1 = (bf16[24,224,256]{2,1,0:T(8,128)(2,1)}, f32[2304,128]{1,0:T(8,128)}) custom-call(bf16[24,2,224,256]{3,2,1,0:T(8,128)(2,1)} %bitcast.4, bf16[48,64,112]{2,1,0:T(8,128)(2,1)} %bitcast.5, bf16[3,3,256,128]{3,2,1,0:T(8,128)(2,1)} %kernel.1), custom_call_target="tpu_custom_call" | custom-call | tf_op jit(solution)/shard_map/grads/pallas_call | solution.py:388
  57.6 4.6 %finish.1 = (bf16[24,2,224,256]{3,2,1,0:T(8,128)(2,1)}, f32[2304,128]{1,0:T(8,128)}) custom-call(bf16[24,224,256]{2,1,0:T(8,128)(2,1)} %get-tuple-element.6.rows, f32[2304,128]{1,0:T(8,128)} %get-tuple-element.7.kg_in), custom_call_target="tpu_custom_call" | custom-call | tf_op jit(solution)/shard_map/finish/pallas_call | solution.py:424

commit v3 on v2

--- a/solution.py
+++ b/solution.py
@@ -12,6 +12,7 @@
 LANES = 128
 F32 = jnp.float32
 BF16 = jnp.bfloat16
+TAP_ORDER = (1, 0, 2)
 AXES = ("lon", "lat", "chan")
 
 
@@ -43,13 +44,15 @@
 def grads_kernel(
     sizes, half_rows, half_cols, out_ch, scale,
     fine, cg, kernel, rows_out, kg_out,
-    fbuf, kcat, tiles, taps, even_t, edge_out, edge_in, acc, rows_buf, row_sem, *rest,
+    fbuf, kcat, tiles, taps, even_t, edge_out, edge_in, spots, acc, rows_buf, row_sem, *rest,
 ):
     landing, (local_sem, tile_recv, tile_send, edge_send, edge_recv, red_send, red_recv, gat_send, gat_recv) = rest[:-9], rest[-9:]
     lon_n, lat_n, chan_n = (sizes[a] for a in AXES)
     me = {a: lax.axis_index(a) for a in AXES}
     lat, chan = me["lat"], me["chan"]
     h = half_rows
+    group = group_size(h + 2)
+    spans = [(max(1, q * group), min(h + 1, (q + 1) * group)) for q in range((h + 2) // group)]
     width = cg.shape[1]
     in_ch = fbuf.shape[2]
     mine = pl.ds(pl.multiple_of(chan * width, width), width)
@@ -70,7 +73,10 @@
 
     is_top = jnp.logical_and(lat == 0, chan == 0)
     is_bottom = jnp.logical_and(lat == lat_n - 1, chan == chan_n - 1)
-    pltpu.make_async_copy(cg.at[pl.ds(chan * h, h)], tiles.at[pl.ds(1, h), mine], tile_recv.at[2]).start()
+    for q, (lo, hi) in enumerate(spans):
+        pltpu.make_async_copy(
+            cg.at[pl.ds(chan * h + lo - 1, hi - lo)], tiles.at[pl.ds(lo, hi - lo), mine], tile_recv.at[2 + q]
+        ).start()
 
     @pl.when(chan > 0)
     def _():
@@ -110,12 +116,7 @@
     for d in range(1, chan_n):
         p = other("chan", d)
         send(p > 0, cg.at[jnp.maximum(p * h - 1, 0)], tiles.at[0, mine], tile_send.at[slot], tile_recv.at[0], {"chan": p})
-        send(None, cg.at[pl.ds(p * h, h)], tiles.at[pl.ds(1, h), mine], tile_send.at[slot + 1], tile_recv.at[2], {"chan": p})
-        send(
-            p < chan_n - 1, cg.at[jnp.minimum((p + 1) * h, chan_n * h - 1)], tiles.at[h + 1, mine],
-            tile_send.at[slot + 2], tile_recv.at[1], {"chan": p},
-        )
-        slot += 3
+        slot += 1
     send(
         lat < lat_n - 1, cg.at[chan_n * h - 1], tiles.at[0, mine], tile_send.at[slot], tile_recv.at[0],
         {"lat": jnp.minimum(lat + 1, lat_n - 1), "chan": 0},
@@ -124,6 +125,22 @@
         lat > 0, cg.at[0], tiles.at[h + 1, mine], tile_send.at[slot + 1], tile_recv.at[1],
         {"lat": jnp.maximum(lat - 1, 0), "chan": chan_n - 1},
     )
+    slot += 2
+    for q, (lo, hi) in enumerate(spans):
+        for d in range(1, chan_n):
+            p = other("chan", d)
+            send(
+                None, cg.at[pl.ds(p * h + lo - 1, hi - lo)], tiles.at[pl.ds(lo, hi - lo), mine],
+                tile_send.at[slot], tile_recv.at[2 + q], {"chan": p},
+            )
+            slot += 1
+    for d in range(1, chan_n):
+        p = other("chan", d)
+        send(
+            p < chan_n - 1, cg.at[jnp.minimum((p + 1) * h, chan_n * h - 1)], tiles.at[h + 1, mine],
+            tile_send.at[slot], tile_recv.at[1], {"chan": p},
+        )
+        slot += 1
 
     local[0].wait()
     pick = one_hot((2 * half_cols, LANES), lambda row, col: row == 2 * col)
@@ -143,15 +160,13 @@
     def _():
         tiles[h + 1] = jnp.zeros(tiles.shape[1:], BF16)
 
-    @pl.when(jnp.logical_not(is_top))
-    def _():
-        pltpu.make_async_copy(tiles.at[0], tiles.at[0], tile_recv.at[0]).wait()
-
-    @pl.when(jnp.logical_not(is_bottom))
-    def _():
-        pltpu.make_async_copy(tiles.at[h + 1], tiles.at[h + 1], tile_recv.at[1]).wait()
-
-    pltpu.make_async_copy(tiles.at[pl.ds(1, h)], tiles.at[pl.ds(1, h)], tile_recv.at[2]).wait()
+    def make_spots(k, _):
+        at = pl.ds(pl.multiple_of(k * LANES, LANES), LANES)
+        for side, lane in ((0, half_cols - 1), (1, 0)):
+            spots[side, :, at] = one_hot((LANES, LANES), lambda row, col: jnp.logical_and(row == k, col == lane))
+        return 0
+
+    lax.fori_loop(0, h + 2, make_spots, 0)
 
     def shifted_source(row, col):
         s, j = col // LANES, col % LANES
@@ -159,49 +174,53 @@
 
     shift = one_hot((half_cols, 3 * LANES), shifted_source)
 
-    def build(k, edges):
-        tile = tiles[k]
-        moved = jnp.dot(tile, shift, preferred_element_type=F32).astype(BF16)
-        at = pl.ds(pl.multiple_of(k * LANES, LANES), LANES)
-        for s in range(3):
-            taps[pl.ds(s * out_ch, out_ch), at] = moved[:, s * LANES:(s + 1) * LANES]
-        last = one_hot(
-            (half_cols, 2 * LANES),
-            lambda row, col: jnp.logical_or(
-                jnp.logical_and(row == half_cols - 1, col == k), jnp.logical_and(row == 0, col == k + LANES)
-            ),
-        )
-        return edges + jnp.dot(tile, last, preferred_element_type=F32)
-
-    edges = lax.fori_loop(0, h + 2, build, jnp.zeros((out_ch, 2 * LANES), F32)).astype(BF16)
-    edge_out[0] = edges[:, :LANES]
-    edge_out[1] = edges[:, LANES:]
+    for q, (lo, hi) in enumerate(spans):
+        if q == 0:
+
+            @pl.when(jnp.logical_not(is_top))
+            def _():
+                pltpu.make_async_copy(tiles.at[0], tiles.at[0], tile_recv.at[0]).wait()
+
+        pltpu.make_async_copy(tiles.at[pl.ds(lo, hi - lo)], tiles.at[pl.ds(lo, hi - lo)], tile_recv.at[2 + q]).wait()
+        if q == len(spans) - 1:
+
+            @pl.when(jnp.logical_not(is_bottom))
+            def _():
+                pltpu.make_async_copy(tiles.at[h + 1], tiles.at[h + 1], tile_recv.at[1]).wait()
+
+        block = tiles[pl.ds(q * group, group)].reshape(group * out_ch, half_cols)
+        moved = jnp.dot(block, shift, preferred_element_type=F32).astype(BF16)
+        for k in range(group):
+            for s in range(3):
+                taps[pl.ds(s * out_ch, out_ch), pl.ds((q * group + k) * LANES, LANES)] = moved[
+                    k * out_ch:(k + 1) * out_ch, s * LANES:(s + 1) * LANES
+                ]
+
+    centre = taps[pl.ds(out_ch, out_ch), :]
+    for side in range(2):
+        edge_out[side] = lax.dot_general(
+            centre, spots[side], (((1,), (1,)), ((), ())), preferred_element_type=F32
+        ).astype(BF16)
     send(None, edge_out.at[0], edge_in.at[0], edge_send.at[0], edge_recv.at[0], {"lon": other("lon", 1)})
     send(None, edge_out.at[1], edge_in.at[1], edge_send.at[1], edge_recv.at[1], {"lon": other("lon", lon_n - 1)})
-    for side in range(2):
-        pltpu.make_async_copy(edge_in.at[side], edge_in.at[side], edge_recv.at[side]).wait()
-
-    def inject(k, _):
-        at = pl.ds(pl.multiple_of(k * LANES, LANES), LANES)
-        for side, s, lane in ((1, 0, half_cols - 1), (0, 2, 0)):
-            spot = one_hot((LANES, LANES), lambda row, col: jnp.logical_and(row == k, col == lane))
-            block = taps[pl.ds(s * out_ch, out_ch), at].astype(F32)
-            block = block + jnp.dot(edge_in[side], spot, preferred_element_type=F32)
-            taps[pl.ds(s * out_ch, out_ch), at] = block.astype(BF16)
-        return 0
-
-    lax.fori_loop(0, h + 2, inject, 0)
+
+    def inject(s, came, spot):
+        pltpu.make_async_copy(edge_in.at[came], edge_in.at[came], edge_recv.at[came]).wait()
+        at = pl.ds(s * out_ch, out_ch)
+        put = jnp.dot(edge_in[came], spots[spot], preferred_element_type=F32)
+        taps[at, :] = (taps[at, :].astype(F32) + put).astype(BF16)
 
     counter = {"red": 0, "gat": 0, "land": 0}
     blocks = reduce_blocks(acc.shape[0], sizes)
     state = []
 
-    def weight_terms(r):
-        part = lax.dot_general(
-            even_t[...], taps[:, (2 - r) * LANES:(2 - r + h) * LANES], (((1,), (1,)), ((), ())), preferred_element_type=F32
-        )
-        for s in range(3):
-            acc[pl.ds((3 * r + s) * in_ch, in_ch), :] = part[:, s * out_ch:(s + 1) * out_ch]
+    def weight_terms(block):
+        s = TAP_ORDER[block]
+        for r in range(3):
+            acc[pl.ds((3 * block + r) * in_ch, in_ch), :] = lax.dot_general(
+                even_t[...], taps[pl.ds(s * out_ch, out_ch), pl.ds((2 - r) * LANES, h * LANES)],
+                (((1,), (1,)), ((), ())), preferred_element_type=F32,
+            )
 
     def owner_of(index, axis, owners):
         if owners == sizes[axis]:
@@ -300,13 +319,15 @@
 
     weight_terms(0)
     scatter(0, 0)
-    weight_terms(1)
+    inject(0, 1, 0)
     add_up(0)
     scatter(0, 1)
+    weight_terms(1)
     scatter(1, 0)
-    weight_terms(2)
+    inject(2, 0, 1)
     add_up(1)
     scatter(1, 1)
+    weight_terms(2)
     scatter(2, 0)
     for copy in local[1:]:
         copy.wait()
@@ -336,18 +357,32 @@
             pl.when(condition)(lambda copy=copy: copy.wait_send())
 
 
+def group_size(slots):
+    return max(size for size in range(1, 14) if slots % size == 0)
+
+
 def reduce_blocks(rows, sizes):
     count = rows // 3
     return [(block * count, stage_plan(count, ("lat", "chan", "lon"), sizes)) for block in range(3)]
 
 
-def finish_kernel(rows, kg_in, grad_out, kg_out, rows_buf, kg_buf, zeros, sems):
+def finish_kernel(rows, kg_in, grad_out, kg_out, rows_buf, kg_buf, zeros, sems, kg_sems):
     zero_rows = zeros.shape[0]
     groups = rows.shape[0] // zero_rows
     kg_read = pltpu.make_async_copy(kg_in, kg_buf, sems.at[0])
-    kg_write = pltpu.make_async_copy(kg_buf, kg_out, sems.at[1])
+    in_ch = kg_in.shape[0] // 9
+    kg_writes = []
+    for block in range(3):
+        for r in range(3):
+            kg_writes.append(
+                pltpu.make_async_copy(
+                    kg_buf.at[pl.ds((3 * block + r) * in_ch, in_ch)],
+                    kg_out.at[pl.ds((3 * r + TAP_ORDER[block]) * in_ch, in_ch)],
+                    kg_sems.at[3 * block + r],
+                )
+            )
     kg_read.start()
-    reads, writes = [], [kg_write]
+    reads, writes = [], list(kg_writes)
     for k in range(groups):
         at = pl.ds(k * zero_rows, zero_rows)
         reads.append(pltpu.make_async_copy(rows.at[at], rows_buf.at[at], sems.at[2 + 3 * k]))
@@ -358,7 +393,8 @@
         writes.append(pltpu.make_async_copy(zeros, grad_out.at[at, 1], sems.at[3 + 3 * k]))
         writes[-1].start()
     kg_read.wait()
-    kg_write.start()
+    for copy in kg_writes:
+        copy.start()
     for k in range(groups):
         at = pl.ds(k * zero_rows, zero_rows)
         reads[k].wait()
@@ -378,6 +414,7 @@
     fine = fine_act.reshape(h, 2, fine_cols, in_ch)
     blocks = reduce_blocks(9 * in_ch, sizes)
     landing, count = [], 0
+    groups = (h + 2) // group_size(h + 2)
     for block, stage in ((0, 0), (0, 1), (1, 0), (1, 1), (2, 0), (2, 1), (0, 2), (1, 2), (2, 2)):
         axis, part, _ = blocks[block][1][stage]
         landing.append(pltpu.VMEM((sizes[axis] - 1, part, out_ch), F32))
@@ -401,13 +438,14 @@
             pltpu.VMEM((in_ch, h * LANES), BF16),
             pltpu.VMEM((2, out_ch, LANES), BF16),
             pltpu.VMEM((2, out_ch, LANES), BF16),
+            pltpu.VMEM((2, LANES, (h + 2) * LANES), BF16),
             pltpu.VMEM((9 * in_ch, out_ch), F32),
             pltpu.VMEM((h, fine_cols, in_ch), BF16),
             dma((4,)),
             *landing,
             dma((10,)),
-            dma((3,)),
-            dma((3 * (chan_n - 1) + 2,)),
+            dma((2 + groups,)),
+            dma(((2 + groups) * (chan_n - 1) + 2,)),
             dma((2,)),
             dma((2,)),
             dma((count,)),
@@ -434,6 +472,7 @@
             pltpu.VMEM(kg.shape, F32),
             pltpu.VMEM((zero_rows, fine_cols, in_ch), BF16),
             dma((2 + 3 * (h // zero_rows),)),
+            dma((9,)),
         ],
         compiler_params=pltpu.CompilerParams(vmem_limit_bytes=60 * 1024 * 1024),
         name="finish",

time: 62.3 us -> 56.2 us (0.902)
  Pallas kernels: 61.5 us -> 55.4 us
    pallas_call x1, Pallas kernels: 56.9 us -> 50.7 us  [on_device(): pl.pallas_call(functools.partial(grads_kernel, sizes, h, w, out_ch, scale...]
where the time goes in v3:
time: 56.2 us; the launch traced here: 56 us
  Pallas kernels  55.4 us (99%)
  between operations  0.64 us (1%)
    pallas_call x1, Pallas kernels, on_device(): pl.pallas_call(functools.partial(grads_kernel, sizes, h, w, out_ch, scale...  50.7 us
    pallas_call x1, Pallas kernels, on_device(): pl.pallas_call(finish_kernel, out_shape=(jax.ShapeDtypeStruct((h, 2, fine...  4.68 us

profile of v3, /device:TPU:0, one launch (start us, length us, event | category | flops | bytes accessed | tf_op | source)
XLA Modules:
  0.0 56.0 jit_solution(11153470076293549310)
XLA Ops:
  0.6 50.7 %grads.1 = (bf16[24,224,256]{2,1,0:T(8,128)(2,1)}, f32[2304,128]{1,0:T(8,128)}) custom-call(bf16[24,2,224,256]{3,2,1,0:T(8,128)(2,1)} %bitcast.4, bf16[48,64,112]{2,1,0:T(8,128)(2,1)} %bitcast.5, bf16[3,3,256,128]{3,2,1,0:T(8,128)(2,1)} %kernel.1), custom_call_target="tpu_custom_call" | custom-call | tf_op jit(solution)/shard_map/grads/pallas_call | solution.py:425
  51.4 4.7 %finish.1 = (bf16[24,2,224,256]{3,2,1,0:T(8,128)(2,1)}, f32[2304,128]{1,0:T(8,128)}) custom-call(bf16[24,224,256]{2,1,0:T(8,128)(2,1)} %get-tuple-element.6.rows, f32[2304,128]{1,0:T(8,128)} %get-tuple-element.7.kg_in), custom_call_target="tpu_custom_call" | custom-call | tf_op jit(solution)/shard_map/finish/pallas_call | solution.py:462

commit v4 on v3

--- a/solution.py
+++ b/solution.py
@@ -327,18 +327,21 @@
     inject(2, 0, 1)
     add_up(1)
     scatter(1, 1)
+    add_up(0)
+    scatter(0, 2)
     weight_terms(2)
     scatter(2, 0)
     for copy in local[1:]:
         copy.wait()
     add_up(2)
     scatter(2, 1)
+    add_up(1)
+    scatter(1, 2)
     even_grads(0)
+    add_up(2)
+    scatter(2, 2)
     for block in range(3):
-        add_up(block)
-        scatter(block, 2)
         even_grads(block + 1)
-    for block in range(3):
         add_up(block, True)
         gather(block, 2)
     for stage in (1, 0):
@@ -415,7 +418,7 @@
     blocks = reduce_blocks(9 * in_ch, sizes)
     landing, count = [], 0
     groups = (h + 2) // group_size(h + 2)
-    for block, stage in ((0, 0), (0, 1), (1, 0), (1, 1), (2, 0), (2, 1), (0, 2), (1, 2), (2, 2)):
+    for block, stage in ((0, 0), (0, 1), (1, 0), (1, 1), (0, 2), (2, 0), (2, 1), (1, 2), (2, 2)):
         axis, part, _ = blocks[block][1][stage]
         landing.append(pltpu.VMEM((sizes[axis] - 1, part, out_ch), F32))
         count += sizes[axis] - 1

time: 56.2 us -> 54.2 us (0.964)
  Pallas kernels: 55.4 us -> 53.5 us
    pallas_call x1, Pallas kernels: 50.7 us -> 48.8 us  [on_device(): pl.pallas_call(functools.partial(grads_kernel, sizes, h, w, out_ch, scale...]
where the time goes in v4:
time: 54.2 us; the launch traced here: 54.1 us
  Pallas kernels  53.5 us (99%)
  between operations  0.64 us (1%)
    pallas_call x1, Pallas kernels, on_device(): pl.pallas_call(functools.partial(grads_kernel, sizes, h, w, out_ch, scale...  48.8 us
    pallas_call x1, Pallas kernels, on_device(): pl.pallas_call(finish_kernel, out_shape=(jax.ShapeDtypeStruct((h, 2, fine...  4.68 us

profile of v4, /device:TPU:0, one launch (start us, length us, event | category | flops | bytes accessed | tf_op | source)
XLA Modules:
  0.0 54.1 jit_solution(9741358035615503043)
XLA Ops:
  0.6 48.8 %grads.1 = (bf16[24,224,256]{2,1,0:T(8,128)(2,1)}, f32[2304,128]{1,0:T(8,128)}) custom-call(bf16[24,2,224,256]{3,2,1,0:T(8,128)(2,1)} %bitcast.4, bf16[48,64,112]{2,1,0:T(8,128)(2,1)} %bitcast.5, bf16[3,3,256,128]{3,2,1,0:T(8,128)(2,1)} %kernel.1), custom_call_target="tpu_custom_call" | custom-call | tf_op jit(solution)/shard_map/grads/pallas_call | solution.py:428
  49.4 4.7 %finish.1 = (bf16[24,2,224,256]{3,2,1,0:T(8,128)(2,1)}, f32[2304,128]{1,0:T(8,128)}) custom-call(bf16[24,224,256]{2,1,0:T(8,128)(2,1)} %get-tuple-element.6.rows, f32[2304,128]{1,0:T(8,128)} %get-tuple-element.7.kg_in), custom_call_target="tpu_custom_call" | custom-call | tf_op jit(solution)/shard_map/finish/pallas_call | solution.py:465
